TPU v7x, 256 devices: a whole 4x4x8 slice. The times are simulated.
256 devices in a mesh: grid: 8 (over y, core), wide: 32 (over z, x).
Axes of the slice: x: 4, y: 4, z: 8, core: 2. Of those that a mesh axis runs over, the one named last changes fastest.
Arguments:
- values: bfloat16 [3584, 64, 4096], P(('grid', 'wide')), may hold values from 0 to 1
- a_block: int32 [3584], P(('grid', 'wide')), may hold values from 0 to 63, as said below
- b_block: int32 [3584], P(('grid', 'wide')), may hold values from 0 to 15
- c_block: int32 [3584], P(('grid', 'wide')), may hold values from 0 to 63
- held: int32 [3584], P(('grid', 'wide')), may hold values from 0 to 1, as said below
- factor_a: bfloat16 [32768, 256], P(('grid', 'wide')), may hold values from -6 to 6
- factor_b: bfloat16 [32768, 256], P(('wide', 'grid')), may hold values from -2.390625 to 2.390625
- factor_c: bfloat16 [4096, 256], replicated, may hold values from -2.390625 to 2.390625
Outputs:
- next_a: float32 [32768, 256], P(('grid', 'wide'))
- next_b: float32 [32768, 256], P(('wide', 'grid'))
- held_loss: float32 [], replicated
Inputs may be any that keep to these rules, and one draw needn't show every extreme that they name: Among the blocks of one device, at most 1 have a_block values with the same a_block // 2; on some device some such value is shared by exactly 1 block. Every device holds 1 to 3 held-out blocks; some device holds exactly 3.
All inputs are finite; a program needn't handle non-finite values.
Results may differ from a plain program's by a relative error of at most 0.0011.
Values may be sent and summed in bfloat16 or wider, within the bound.
No kernel may reach another device: no remote copies, remote signals or barrier semaphores. Data moves between devices by JAX's collectives and lax.ppermute only.
A program may use at most 64 MiB of HBM per device.

v0:
```python
import jax
import jax.numpy as jnp
from jax import lax
from jax.sharding import PartitionSpec as P

step_size = 0.05


def block_terms(inputs):
    entries, a_rows, b_rows, c_rows, flag = inputs
    side = a_rows.shape[0]
    width = a_rows.shape[1]
    khatri = (
        b_rows.astype(jnp.float32)[:, None, :] * c_rows.astype(jnp.float32)[None, :, :]
    ).astype(jnp.bfloat16)
    khatri = khatri.reshape(side * side, width)
    model = lax.dot_general(
        a_rows, khatri, (((1,), (1,)), ((), ())), preferred_element_type=jnp.float32
    )
    entry_f = entries.astype(jnp.float32)
    resid = ((jax.nn.sigmoid(model) - entry_f) * (1.0 - flag)).astype(jnp.bfloat16)
    loss_part = jnp.sum(jax.nn.softplus(model) - entry_f * model) * flag
    grad_rows = jnp.dot(resid, khatri, preferred_element_type=jnp.float32)
    partial_sum = lax.dot_general(
        resid, a_rows, (((0,), (0,)), ((), ())), preferred_element_type=jnp.float32
    )
    grad_cols = jnp.sum(
        partial_sum.reshape(side, side, width) * c_rows.astype(jnp.float32)[None, :, :], axis=1
    )
    return (grad_rows, grad_cols, loss_part)


def per_device(values, a_block, b_block, c_block, held, factor_a, factor_b, factor_c):
    blocks = values.shape[0]
    side = values.shape[1]
    width = factor_a.shape[1]
    highest = lax.Precision.HIGHEST
    own_blocks = factor_a.shape[0] // side
    wide_count = lax.axis_size("wide")
    b_panel = lax.all_gather(factor_b, "grid", axis=0, tiled=True)
    b_rows = b_panel.reshape(-1, side, width)[b_block]
    c_rows = factor_c.reshape(-1, side, width)[c_block]
    a_panel = lax.all_gather(factor_a, "wide", axis=0, tiled=True)
    a_rows = a_panel.reshape(-1, side, width)[a_block]
    flags = held.astype(jnp.float32)
    grad_rows, grad_cols, loss_parts = lax.map(block_terms, (values, a_rows, b_rows, c_rows, flags))
    panel_blocks = own_blocks * wide_count
    matches = (a_block[:, None] == jnp.arange(panel_blocks)[None, :]).astype(jnp.float32)
    panel_grad = jnp.einsum("np,nk->pk", matches, grad_rows.reshape(blocks, -1), precision=highest)
    grad_a = lax.psum_scatter(
        panel_grad.reshape(panel_blocks * side, width), "wide", scatter_dimension=0, tiled=True
    )
    b_panel_blocks = b_panel.shape[0] // side
    b_matches = (b_block[:, None] == jnp.arange(b_panel_blocks)[None, :]).astype(jnp.float32)
    b_panel_grad = jnp.einsum(
        "np,nk->pk", b_matches, grad_cols.reshape(blocks, -1), precision=highest
    )
    grad_b = lax.psum_scatter(
        b_panel_grad.reshape(b_panel_blocks * side, width), "grid", scatter_dimension=0, tiled=True
    )
    loss_total, held_total = lax.psum((jnp.sum(loss_parts), jnp.sum(flags)), ("grid", "wide"))
    held_loss = loss_total / (held_total * (side * side * side))
    next_a = factor_a.astype(jnp.float32) - step_size * grad_a
    next_b = factor_b.astype(jnp.float32) - step_size * grad_b
    return (next_a, next_b, held_loss)


def solution(mesh):
    in_specs = (
        P(("grid", "wide"), None, None),
        P(("grid", "wide")),
        P(("grid", "wide")),
        P(("grid", "wide")),
        P(("grid", "wide")),
        P(("grid", "wide"), None),
        P(("wide", "grid"), None),
        P(),
    )
    out_specs = (P(("grid", "wide"), None), P(("wide", "grid"), None), P())
    return jax.shard_map(
        per_device, mesh=mesh, in_specs=in_specs, out_specs=out_specs, check_vma=False
    )
```

profile of v0, /device:TPU:16, one launch (start us, length us, event | category | flops | bytes accessed | tf_op | source)
XLA Modules:
  0.0 561.8 jit_solution(8834478500784365606)
XLA Ops:
  10.6 13.3 %all_gather.7 = bf16[1024,256]{1,0:T(8,128)(2,1)S(1)} all-gather(bf16[128,256]{1,0:T(8,128)(2,1)} %param.16), channel_id=1, replica_groups=mesh['grid'=8,'wide'=32] {'grid'}, dimensions={0}, use_global_device_ids=true | all-gather | bytes 589824 | tf_op jit(solution)/shard_map/all_gather | solution.py:40
  25.2 66.1 %all-gather.2.cloned.1.call-done = bf16[4096,256]{1,0:T(8,128)(2,1)} async-done(((bf16[128,256]{1,0:T(8,128)(2,1)}), bf16[4096,256]{1,0:T(8,128)(2,1)}) %all-gather.2.cloned.1.call-update) | async-done | bytes 2097168 | tf_op jit(solution)/shard_map/all_gather | solution.py:43
  91.3 2.9 gather_fusion
  94.2 195.9 %while.14 = (s32[]{:T(128)}, f32[14,64,256]{2,1,0:T(8,128)}, f32[14,64,256]{2,1,0:T(8,128)}, f32[14]{0:T(128)S(1)}, bf16[14,64,256]{2,1,0:T(8,128)(2,1)}, /*inde...) while((s32[]{:T(128)}, f32[14,64,256]{2,1,0:T(8,128)}, ...), condition=%wide.region_3.4_spmd, body=%wide.region_0.3_spmd.sunk | while | flops 411058176 | bytes 19072724 | solution.py:46
  96.9 3.3 fusion.34
  110.9 3.3 fusion.34
  124.9 3.3 fusion.34
  138.9 3.3 fusion.34
  152.9 3.3 fusion.34
  157.5 2.7 fusion.35
  166.9 3.3 fusion.34
  180.9 3.3 fusion.34
  194.9 3.3 fusion.34
  208.9 3.3 fusion.34
  222.8 3.3 fusion.34
  236.8 3.3 fusion.34
  250.8 3.3 fusion.34
  255.4 2.7 fusion.35
  264.8 3.3 fusion.34
  278.8 3.3 fusion.34
  295.9 3.9 fusion.12
  299.8 4.9 reshape.59
  306.6 73.8 %all-reduce = (f32[]{:T(128)}, f32[]{:T(128)}) all-reduce(f32[]{:T(128)} %reduce_sum.36, f32[]{:T(128)} %convert_reduce_fusion), channel_id=1, replica_groups=mesh['grid'=8,'wide'=32] {'grid','wide'}, use_global_device_ids=true, to_apply=%region_7.8 | all-reduce | flops 2 | bytes 16 | tf_op jit(solution)/shard_map/psum | solution.py:61
  383.4 169.2 %reduce-scatter.3.cloned.1.call-done = f32[128,256]{1,0:T(8,128)} async-done(((f32[4096,256]{1,0:T(8,128)}), f32[128,256]{1,0:T(8,128)}) %reduce-scatter.3.cloned.1.call-update) | async-done | bytes 131088 | tf_op jit(solution)/shard_map/reduce_scatter | solution.py:50
  (179 shorter events, 132.0 us)
Async XLA Ops:
  7.2 2.2 copy-start
  7.2 18.0 %copy-start.5 = (s32[14]{0:T(128)S(1)}, s32[14]{0:T(128)}, u32[]{:S(2)}) copy-start(s32[14]{0:T(128)} %param.11) | copy-start | bytes 172
  7.2 84.1 %all-gather.2.cloned.1.call-start = ((), (), s32[]{:S(2)}) async-start(), calls=%async_computation.2 | async-start | bytes 2162688 | tf_op jit(solution)/shard_map/all_gather | solution.py:43
  7.9 373.8 %reduce-scatter.5.cloned.1.call-start = ((), (), s32[]{:S(2)}) async-start(), calls=%async_computation.4 | async-start | bytes 1179648 | tf_op jit(solution)/shard_map/reduce_scatter | solution.py:58
  96.9 3.3 copy-start.1
  110.9 3.3 copy-start.1
  124.9 3.3 copy-start.1
  138.9 3.3 copy-start.1
  152.9 3.3 copy-start.1
  166.9 3.3 copy-start.1
  180.9 3.3 copy-start.1
  194.9 3.3 copy-start.1
  208.9 3.3 copy-start.1
  222.8 3.3 copy-start.1
  236.8 3.3 copy-start.1
  250.8 3.3 copy-start.1
  264.8 3.3 copy-start.1
  278.8 3.3 copy-start.1
  290.1 1.9 copy-start.4
  294.0 258.6 %reduce-scatter.3.cloned.1.call-start = ((), (), s32[]{:S(2)}) async-start(), calls=%async_computation.3 | async-start | bytes 4325376 | tf_op jit(solution)/shard_map/reduce_scatter | solution.py:50
  304.7 0.7 copy-start.6
  304.7 77.0 %copy-start.2 = (bf16[128,256]{1,0:T(8,128)(2,1)S(1)}, bf16[128,256]{1,0:T(8,128)(2,1)}, u32[]{:S(2)}) copy-start(bf16[128,256]{1,0:T(8,128)(2,1)} %param.16) | copy-start | bytes 196612
  304.7 247.9 %copy-start.3 = (bf16[128,256]{1,0:T(8,128)(2,1)S(1)}, bf16[128,256]{1,0:T(8,128)(2,1)}, u32[]{:S(2)}) copy-start(bf16[128,256]{1,0:T(8,128)(2,1)} %param.15) | copy-start | bytes 196612
Sparse Core Ops, SparseCore 0:
  10.6 80.6 all-gather.1
  294.1 27.0 reduce-scatter.4
  325.1 227.4 reduce-scatter.2
where the time goes:
time: 565 us; the launch traced here: 562 us
  waiting for transfers between devices  236 us (42%)
  matrix products  115 us (20%)
  blocking collectives  87.1 us (15%)
  local copies, waits for them, and re-layouts  52.6 us (9%)
  loops' own time  27.7 us (5%)
  other arithmetic  26.8 us (5%)
  between operations  16.3 us (3%)
    reduce_scatter x1, waiting for transfers between devices, per_device(): lax.psum_scatter(panel_grad.reshape(panel_blocks * side, width), 'wide',...  169 us
    psum x1, blocking collectives, per_device(): lax.psum((jnp.sum(loss_parts), jnp.sum(flags)), ('grid', 'wide'))  73.8 us
    all_gather x1, waiting for transfers between devices, per_device(): a_panel = lax.all_gather(factor_a, 'wide', axis=0, tiled=True)  66.1 us
    dot_general x14, matrix products, block_terms(): lax.dot_general(a_rows, khatri, (((1,), (1,)), ((), ())), preferred_eleme...  46.2 us
    dot_general x14, matrix products, block_terms(): grad_rows = jnp.dot(resid, khatri, preferred_element_type=jnp.float32)  37.5 us
    another operation x1, loops' own time, per_device(): lax.map(block_terms, (values, a_rows, b_rows, c_rows, flags))  27.7 us
    dot_general x14, matrix products, block_terms(): lax.dot_general(resid, a_rows, (((0,), (0,)), ((), ())), preferred_elemen...  26.9 us
    dot_general x14, local copies, waits for them, and re-layouts, block_terms(): lax.dot_general(resid, a_rows, (((0,), (0,)), ((), ())), preferred_elemen...  18.7 us
  transfers between devices with their start and end apart: 3, of which 2 were waited for; matrix products, arithmetic and copies ran while one was open for 3% of the time, Pallas kernels for 0%

commit v1 on v0

v1 whole, which is shorter than its diff:
```python
import jax
import jax.numpy as jnp
from jax import lax
from jax.experimental import pallas as pl
from jax.experimental.pallas import tpu as pltpu
from jax.sharding import PartitionSpec as P

step_size = 0.05
chunk_rows = 8


def block_kernel(slot_at, b_at, c_at, held, values, a_rows, b_rows, c_rows, out_a, out_b):
    step = pl.program_id(0)
    side = a_rows.shape[1]
    width = a_rows.shape[2]
    span = chunk_rows * side
    pair = out_b.shape[1] - 8
    a = a_rows[0]
    c_wide = c_rows[0].astype(jnp.float32)

    @pl.when(step == 0)
    def _():
        out_a[...] = jnp.zeros_like(out_a)
        out_b[...] = jnp.zeros_like(out_b)

    def chunk(i):
        b = b_rows[0, pl.ds(i * chunk_rows, chunk_rows), :].astype(jnp.float32)
        khatri = (b[:, None, :] * c_wide[None, :, :]).astype(jnp.bfloat16).reshape(span, width)
        model = lax.dot_general(
            a, khatri, (((1,), (1,)), ((), ())), preferred_element_type=jnp.float32
        )
        return khatri, model, values[0, :, pl.ds(i * span, span)].astype(jnp.float32)

    @pl.when(held[step] == 1)
    def _():
        total = jnp.zeros((8, 128), jnp.float32)
        for i in range(side // chunk_rows):
            khatri, model, entry = chunk(i)
            soft = jnp.maximum(model, 0.0) + jnp.log1p(jnp.exp(-jnp.abs(model)))
            part = jnp.sum((soft - entry * model).reshape(side // 8, 8, span), axis=0)
            for j in range(span // 128):
                total = total + part[:, j * 128 : (j + 1) * 128]
        for g in range(out_b.shape[0]):
            out_b[g, pair:, 0:128] += total
            out_b[g, pair:, 128:256] += jnp.full((8, 128), 1.0 / 1024.0, jnp.float32)

    @pl.when(held[step] == 0)
    def _():
        acc = jnp.zeros((side, width), jnp.float32)
        where_b = b_at[step]
        group = where_b // 2
        base = (where_b % 2) * side
        for i in range(side // chunk_rows):
            khatri, model, entry = chunk(i)
            resid = (jax.nn.sigmoid(model) - entry).astype(jnp.bfloat16)
            acc = acc + jnp.dot(resid, khatri, preferred_element_type=jnp.float32)
            part = lax.dot_general(
                resid, a, (((0,), (0,)), ((), ())), preferred_element_type=jnp.float32
            )
            cols = jnp.sum(part.reshape(chunk_rows, side, width) * c_wide[None, :, :], axis=1)
            spot = pl.multiple_of(base + i * chunk_rows, 8)
            out_b[group, pl.ds(spot, chunk_rows), :] += cols
        out_a[slot_at[step]] = acc


def per_device(values, a_block, b_block, c_block, held, factor_a, factor_b, factor_c):
    blocks, side, entries = values.shape
    width = factor_a.shape[1]
    wide_count = lax.axis_size("wide")
    grid_count = lax.axis_size("grid")
    b_panel = lax.all_gather(factor_b, "grid", axis=0, tiled=True).reshape(-1, side, width)
    slot = a_block // 2
    within = a_block % 2
    matches = slot[None, :] == jnp.arange(wide_count, dtype=jnp.int32)[:, None]
    wanted = jnp.sum(jnp.where(matches, within[None, :], 0), axis=1)
    asked = lax.all_to_all(
        jnp.broadcast_to(wanted[:, None, None], (wide_count, 1, 128)), "wide", 0, 0
    )[:, 0, 0]
    second = (asked == 1)[:, None, None]
    own_a = factor_a.reshape(2, side, width)
    a_slots = lax.all_to_all(
        jnp.where(second, own_a[1][None], own_a[0][None]), "wide", 0, 0
    )
    pick = lambda array_of: pl.BlockSpec((1, side, width), array_of)
    out_a, out_b = pl.pallas_call(
        block_kernel,
        grid_spec=pltpu.PrefetchScalarGridSpec(
            num_scalar_prefetch=4,
            grid=(blocks,),
            in_specs=[
                pl.BlockSpec((1, side, entries), lambda i, s, b, c, h: (i, 0, 0)),
                pick(lambda i, s, b, c, h: (s[i], 0, 0)),
                pick(lambda i, s, b, c, h: (b[i], 0, 0)),
                pick(lambda i, s, b, c, h: (c[i], 0, 0)),
            ],
            out_specs=[
                pl.BlockSpec((wide_count, side, width), lambda i, s, b, c, h: (0, 0, 0)),
                pl.BlockSpec((grid_count, 2 * side + 8, width), lambda i, s, b, c, h: (0, 0, 0)),
            ],
        ),
        out_shape=[
            jax.ShapeDtypeStruct((wide_count, side, width), jnp.float32),
            jax.ShapeDtypeStruct((grid_count, 2 * side + 8, width), jnp.float32),
        ],
        cost_estimate=pl.CostEstimate(
            flops=6 * blocks * side * entries * width,
            bytes_accessed=2 * blocks * side * entries,
            transcendentals=blocks * side * entries,
        ),
    )(slot, b_block, c_block, held, values, a_slots, b_panel, factor_c.reshape(-1, side, width))
    got_b = lax.all_to_all(out_b, "grid", 0, 0)
    grad_b = jnp.sum(got_b, axis=0)
    tail = grad_b[2 * side :]
    sums = jnp.stack([jnp.sum(tail[:, :128]), jnp.sum(tail[:, 128:])])
    spread = jnp.broadcast_to(jnp.repeat(sums, 64)[None, None, :], (wide_count, 1, 128))
    every = jnp.sum(lax.all_to_all(spread, "wide", 0, 0)[:, 0, :], axis=0)
    held_loss = every[0] / (every[64] * (side * side * side))
    got_a = lax.all_to_all(out_a, "wide", 0, 0)
    first_sum = jnp.sum(jnp.where(second, 0.0, got_a), axis=0)
    second_sum = jnp.sum(jnp.where(second, got_a, 0.0), axis=0)
    grad_a = jnp.concatenate([first_sum, second_sum], axis=0)
    next_a = factor_a.astype(jnp.float32) - step_size * grad_a
    next_b = factor_b.astype(jnp.float32) - step_size * grad_b[: 2 * side]
    return (next_a, next_b, held_loss)


def solution(mesh):
    in_specs = (
        P(("grid", "wide"), None, None),
        P(("grid", "wide")),
        P(("grid", "wide")),
        P(("grid", "wide")),
        P(("grid", "wide")),
        P(("grid", "wide"), None),
        P(("wide", "grid"), None),
        P(),
    )
    out_specs = (P(("grid", "wide"), None), P(("wide", "grid"), None), P())
    return jax.shard_map(
        per_device, mesh=mesh, in_specs=in_specs, out_specs=out_specs, check_vma=False
    )
```

time: 565 us -> 191 us (0.34)
  waiting for transfers between devices: 236 us -> 70.1 us
  matrix products: 115 us -> 0 us
  local copies, waits for them, and re-layouts: 52.6 us -> 3.25 us
  blocking collectives: 87.1 us -> 49.8 us
  Pallas kernels: 0 us -> 36.8 us
  loops' own time: 27.7 us -> 0 us
  other arithmetic: 26.8 us -> 6.39 us
  starting transfers between devices: 0.12 us -> 19.3 us
  between operations: 16.3 us -> 3.15 us
    reduce_scatter x2 -> x0, waiting for transfers between devices: 169 us -> none  [the longest x1 169 us: per_device(): lax.psum_scatter(panel_grad.reshape(panel_blocks * side, width), 'wide',...]
    dot_general x44 -> x0, matrix products: 115 us -> none  [the longest x14 46.2 us: block_terms(): lax.dot_general(a_rows, khatri, (((1,), (1,)), ((), ())), preferred_eleme...]
    psum x1 -> x0, blocking collectives: 73.8 us -> none  [per_device(): lax.psum((jnp.sum(loss_parts), jnp.sum(flags)), ('grid', 'wide'))]
    all_to_all x0 -> x3, waiting for transfers between devices: none -> 70.1 us  [the longest x1 47 us: per_device(): got_a = lax.all_to_all(out_a, 'wide', 0, 0)]
    all_gather x1 -> x0, waiting for transfers between devices: 66.1 us -> none  [per_device(): a_panel = lax.all_gather(factor_a, 'wide', axis=0, tiled=True)]
    all_to_all x0 -> x2, blocking collectives: none -> 36.8 us  [the longest x1 19 us: per_device(): got_b = lax.all_to_all(out_b, 'grid', 0, 0)]
    pallas_call x0 -> x1, Pallas kernels: none -> 36.8 us  [per_device(): pl.pallas_call(block_kernel, grid_spec=pltpu.PrefetchScalarGridSpec(num_s...]
    another operation x1 -> x0, loops' own time: 27.7 us -> none  [per_device(): lax.map(block_terms, (values, a_rows, b_rows, c_rows, flags))]
  transfers between devices with their start and end apart: 3 -> 3, of which waited for: 2 -> 3; matrix products, arithmetic and copies ran while one was open for 3% -> 1% of each run, Pallas kernels for 0% -> 0%
where the time goes in v1:
time: 191 us; the launch traced here: 189 us
  waiting for transfers between devices  70.1 us (37%)
  blocking collectives  49.8 us (26%)
  Pallas kernels  36.8 us (19%)
  starting transfers between devices  19.3 us (10%)
  other arithmetic  6.39 us (3%)
  local copies, waits for them, and re-layouts  3.25 us (2%)
  between operations  3.15 us (2%)
    all_to_all x1, waiting for transfers between devices, per_device(): got_a = lax.all_to_all(out_a, 'wide', 0, 0)  47 us
    pallas_call x1, Pallas kernels, per_device(): pl.pallas_call(block_kernel, grid_spec=pltpu.PrefetchScalarGridSpec(num_s...  36.8 us
    all_to_all x1, blocking collectives, per_device(): got_b = lax.all_to_all(out_b, 'grid', 0, 0)  19 us
    all_to_all x1, blocking collectives, per_device(): every = jnp.sum(lax.all_to_all(spread, 'wide', 0, 0)[:, 0, :], axis=0)  17.8 us
    all_to_all x1, waiting for transfers between devices, per_device(): lax.all_to_all(jnp.where(second, own_a[1][None], own_a[0][None]), 'wide',...  14.2 us
    all_gather x1, blocking collectives, per_device(): lax.all_gather(factor_b, 'grid', axis=0, tiled=True)  13 us
    all_to_all x1, starting transfers between devices, per_device(): lax.all_to_all(jnp.broadcast_to(wanted[:, None, None], (wide_count, 1, 12...  11.3 us
    all_to_all x1, waiting for transfers between devices, per_device(): lax.all_to_all(jnp.broadcast_to(wanted[:, None, None], (wide_count, 1, 12...  8.9 us
  transfers between devices with their start and end apart: 3, of which 3 were waited for; matrix products, arithmetic and copies ran while one was open for 1% of the time, Pallas kernels for 0%

profile of v1, /device:TPU:16, one launch (start us, length us, event | category | flops | bytes accessed | tf_op | source)
XLA Modules:
  0.0 188.7 jit_solution(17906539501149165247)
XLA Ops:
  0.6 0.7 and_select_fusion
  1.3 0.1 select_reduce_fusion.2
  1.4 0.7 broadcast_in_dim.78
  2.1 11.3 %all-to-all-start = ((s32[32,1,128]{2,1,0:T(1,128)}), s32[32,1,128]{2,1,0:T(1,128)S(1)}, u32[]{:S(2)}, u32[]{:S(2)}) async-start(s32[32,1,128]{2,1,0:T(1,128)} %broadcast_in_dim.78), calls=%async_computation | async-start | bytes 32768 | tf_op jit(solution)/shard_map/all_to_all | solution.py:76
  13.5 0.8 fusion.2
  14.2 8.9 %all-to-all-done = s32[32,1,128]{2,1,0:T(1,128)S(1)} async-done(((s32[32,1,128]{2,1,0:T(1,128)}), s32[32,1,128]{2,1,0:T(1,128)S(1)}, u32[]{:S(2)}, u32[]{:S(2)}) %all-to-all-start) | async-done | bytes 16416 | tf_op jit(solution)/shard_map/all_to_all | solution.py:76
  23.1 0.7 compare_reduce_fusion
  23.8 1.1 broadcast_select_fusion
  24.9 3.9 %all-to-all-start.1 = ((bf16[32,64,256]{2,1,0:T(8,128)(2,1)}), bf16[32,64,256]{2,1,0:T(8,128)(2,1)S(1)}, u32[]{:S(2)}, u32[]{:S(2)}) async-start(bf16[32,64,256]{2,1,0:T(8,128)(2,1)} %broadcast_select_fusion), calls=%async_computation.1 | async-start | bytes 2097152 | tf_op jit(solution)/shard_map/all_to_all | solution.py:81
  28.9 13.0 %all_gather.3 = bf16[1024,256]{1,0:T(8,128)(2,1)} all-gather(bf16[128,256]{1,0:T(8,128)(2,1)S(1)} %copy-done.1), channel_id=1, replica_groups=mesh['grid'=8,'wide'=32] {'grid'}, dimensions={0}, use_global_device_ids=true | all-gather | bytes 589824 | tf_op jit(solution)/shard_map/all_gather | solution.py:71
  41.9 14.2 %all-to-all-done.1.a_rows = bf16[32,64,256]{2,1,0:T(8,128)(2,1)S(1)} async-done(((bf16[32,64,256]{2,1,0:T(8,128)(2,1)}), bf16[32,64,256]{2,1,0:T(8,128)(2,1)S(1)}, u32[]{:S(2)}, u32[]{:S(2)}) %all-to-all-start.1) | async-done | bytes 1048608 | tf_op jit(solution)/shard_map/all_to_all | solution.py:81
  56.1 1.0 copy-done
  57.1 36.8 %shard_map.103 = (f32[32,64,256]{2,1,0:T(8,128)}, f32[8,136,256]{2,1,0:T(8,128)}) custom-call(s32[14]{0:T(128)} %copy-done.3, s32[14]{0:T(128)} %b_at.1, s32[14]{0:T(128)} %c_at.1, s32[14]{0:T(128)} %held.1, bf16[14,64,4096]{2,1,0:T(8,128)(2,1)} %values.1, bf16[32,64,256]{2,1,0:T(8,128)(2,1)} %copy-done, bf16[16,64,256]{2,1,0:T(8,128)(2,1)} %bitcast.6, ...), custom_call_target="tpu_custom_call" | custom-call | flops 5637144576 | bytes 7340032 | tf_op jit(solution)/shard_map/pallas_call | solution.py:85
  93.8 19.0 %all_to_all.25 = f32[8,136,256]{2,1,0:T(8,128)S(1)} all-to-all(f32[8,136,256]{2,1,0:T(8,128)} %get-tuple-element.6), channel_id=1, replica_groups=mesh['grid'=8,'wide'=32] {'grid'}, dimensions={0} | all-to-all | bytes 2228224 | tf_op jit(solution)/shard_map/all_to_all | solution.py:111
  112.9 0.6 slice_reduce_fusion.1
  113.5 1.4 pad_maximum_fusion
  115.0 0.1 broadcast_in_dim.85
  115.1 17.8 %all_to_all.26 = f32[32,1,128]{2,1,0:T(1,128)S(1)} all-to-all(f32[32,1,128]{2,1,0:T(1,128)S(1)} %broadcast_in_dim.86), channel_id=1, replica_groups=mesh['grid'=8,'wide'=32] {'wide'}, dimensions={0} | all-to-all | bytes 32768 | tf_op jit(solution)/shard_map/all_to_all | solution.py:116
  132.8 4.0 %all-to-all-start.2 = ((f32[32,64,256]{2,1,0:T(8,128)}), f32[32,64,256]{2,1,0:T(8,128)S(1)}, u32[]{:S(2)}, u32[]{:S(2)}) async-start(f32[32,64,256]{2,1,0:T(8,128)} %get-tuple-element.5), calls=%async_computation.2 | async-start | bytes 4194304 | tf_op jit(solution)/shard_map/all_to_all | solution.py:118
  136.9 0.7 fusion
  137.6 0.6 fusion.3
  139.5 47.0 %all-to-all-done.2 = f32[32,64,256]{2,1,0:T(8,128)S(1)} async-done(((f32[32,64,256]{2,1,0:T(8,128)}), f32[32,64,256]{2,1,0:T(8,128)S(1)}, u32[]{:S(2)}, u32[]{:S(2)}) %all-to-all-start.2) | async-done | bytes 2097184 | tf_op jit(solution)/shard_map/all_to_all | solution.py:118
  186.4 0.4 select_reduce_fusion.1
  186.9 0.7 fusion.1
  (11 shorter events, 0.2 us)
Async XLA Ops:
  0.6 28.3 %copy-start.1 = (bf16[128,256]{1,0:T(8,128)(2,1)S(1)}, bf16[128,256]{1,0:T(8,128)(2,1)}, u32[]{:S(2)}) copy-start(bf16[128,256]{1,0:T(8,128)(2,1)} %param.14) | copy-start | bytes 196612
  1.3 54.8 %copy-start.3 = (s32[14]{0:T(128)}, s32[14]{0:T(128)S(1)}, u32[]{:S(2)}) copy-start(s32[14]{0:T(128)S(1)} %get-tuple-element.16.slot_at) | copy-start | bytes 172
  2.1 21.0 %all-to-all-start = ((s32[32,1,128]{2,1,0:T(1,128)}), s32[32,1,128]{2,1,0:T(1,128)S(1)}, u32[]{:S(2)}, u32[]{:S(2)}) async-start(s32[32,1,128]{2,1,0:T(1,128)} %broadcast_in_dim.78), calls=%async_computation | async-start | bytes 32768 | tf_op jit(solution)/shard_map/all_to_all | solution.py:76
  24.9 31.2 %all-to-all-start.1 = ((bf16[32,64,256]{2,1,0:T(8,128)(2,1)}), bf16[32,64,256]{2,1,0:T(8,128)(2,1)S(1)}, u32[]{:S(2)}, u32[]{:S(2)}) async-start(bf16[32,64,256]{2,1,0:T(8,128)(2,1)} %broadcast_select_fusion), calls=%async_computation.1 | async-start | bytes 2097152 | tf_op jit(solution)/shard_map/all_to_all | solution.py:81
  56.1 1.0 copy-start
  132.8 53.6 %all-to-all-start.2 = ((f32[32,64,256]{2,1,0:T(8,128)}), f32[32,64,256]{2,1,0:T(8,128)S(1)}, u32[]{:S(2)}, u32[]{:S(2)}) async-start(f32[32,64,256]{2,1,0:T(8,128)} %get-tuple-element.5), calls=%async_computation.2 | async-start | bytes 4194304 | tf_op jit(solution)/shard_map/all_to_all | solution.py:118
  136.9 50.0 %copy-start.2 = (bf16[128,256]{1,0:T(8,128)(2,1)S(1)}, bf16[128,256]{1,0:T(8,128)(2,1)}, u32[]{:S(2)}) copy-start(bf16[128,256]{1,0:T(8,128)(2,1)} %param.13) | copy-start | bytes 196612
